TPU v7x, 128 devices: a whole 4x4x4 slice. The times are simulated.
128 devices in a mesh: rep: 4 (over y_hi, core), fsdp: 32 (over z, y_lo, x).
Axes of the slice: x: 4, y: 4 (y_hi: 2, y_lo: 2; y = y_hi * 2 + y_lo), z: 4, core: 2. Of those that a mesh axis runs over, the one named last changes fastest.
Arguments:
- tokens: bfloat16 [16384, 1088], P(('rep', 'fsdp')), may hold values from -6 to 6
- segments: int32 [16384], P(('rep', 'fsdp')), may hold values from 0 to 101, as said below
- ln_gain: bfloat16 [1, 2, 1088], P(None, None, 'fsdp'), may hold values from 0.099609375 to 1.8984375
- ln_bias: bfloat16 [1, 2, 1088], P(None, None, 'fsdp'), may hold values from -1.75 to 1.75
- w_qkv: bfloat16 [1, 1088, 3264], P(None, 'fsdp'), may hold values from -1 to 1
- w_out: bfloat16 [1, 1088, 1088], P(None, 'fsdp'), may hold values from -0.5 to 0.5
- w_fc1: bfloat16 [1, 1088, 4352], P(None, 'fsdp'), may hold values from -0.1875 to 0.1875
- w_fc2: bfloat16 [1, 4352, 1088], P(None, 'fsdp'), may hold values from -0.09375 to 0.09375
- cotangent: bfloat16 [16384, 1088], P(('rep', 'fsdp')), may hold values from -6 to 6
Outputs:
- block_output: bfloat16 [16384, 1088], P(('rep', 'fsdp'))
- grad_tokens: float32 [16384, 1088], P(('rep', 'fsdp'))
- grad_ln_gain: float32 [1, 2, 1088], P(None, None, 'fsdp')
- grad_ln_bias: float32 [1, 2, 1088], P(None, None, 'fsdp')
- grad_qkv: float32 [1, 1088, 3264], P(None, 'fsdp')
- grad_out: float32 [1, 1088, 1088], P(None, 'fsdp')
- grad_fc1: float32 [1, 1088, 4352], P(None, 'fsdp')
- grad_fc2: float32 [1, 4352, 1088], P(None, 'fsdp')
Inputs may be any that keep to these rules, and one draw needn't show every extreme that they name: `segments`: segment numbers never fall along the token stream and each number from 0 to the most is used; a document is a run of equal numbers, 20 to 300 tokens long before sequence ends cut it.
All inputs are finite; a program needn't handle non-finite values.
Results may differ from a plain program's by a relative error of at most 0.025.
Values may be sent and summed in bfloat16 or wider, within the bound.
A program may use at most 192 MiB of HBM per device.

v0:
```python
import jax
import jax.numpy as jnp
from jax import lax
from jax.sharding import PartitionSpec as P

D = 1088
HEADS = 17
HEAD_DIM = 64
SEQ = 128
LAYERS = 1
EPS = 1e-05


def normalize(resid_in, gain_full, bias_full):
    feat_mean = jnp.mean(resid_in, axis=-1, keepdims=True)
    centred = resid_in - feat_mean
    feat_var = jnp.mean(centred * centred, axis=-1, keepdims=True)
    return centred * lax.rsqrt(feat_var + EPS) * gain_full + bias_full


def cross_rows(left_op, right_op):
    return lax.dot_general(
        left_op, right_op, (((0,), (0,)), ((), ())), preferred_element_type=jnp.float32
    )


def against(left_op, right_op):
    return lax.dot_general(
        left_op, right_op, (((1,), (1,)), ((), ())), preferred_element_type=jnp.float32
    )


def product(pattern, left_op, right_op):
    return jnp.einsum(pattern, left_op, right_op, preferred_element_type=jnp.float32)


def allowed_mask(seg_block):
    positions = jnp.arange(seg_block.shape[1])
    causal = positions[:, None] >= positions[None, :]
    same_doc = seg_block[:, :, None] == seg_block[:, None, :]
    return (causal[None] & same_doc)[:, None]


def scores_of(query_part, key_part, allowed):
    scores = product("sqhe,skhe->shqk", query_part, key_part) * 0.125
    return jnp.where(allowed, scores, -1e30)


def forward_layer(resid_in, allowed, whole_set):
    gain, bias, w_query, w_proj, w_first, w_second = whole_set
    row_count = resid_in.shape[0]
    seq_count = row_count // SEQ
    gain_full = gain.astype(jnp.float32)
    bias_full = bias.astype(jnp.float32)
    normed_one = normalize(resid_in, gain_full[0], bias_full[0]).astype(jnp.bfloat16)
    proj_qkv = jnp.dot(normed_one, w_query, preferred_element_type=jnp.float32).astype(jnp.bfloat16)
    proj_qkv = proj_qkv.reshape(seq_count, SEQ, 3, HEADS, HEAD_DIM)
    scores = scores_of(proj_qkv[:, :, 0], proj_qkv[:, :, 1], allowed)
    row_max = jnp.max(scores, axis=-1, keepdims=True)
    log_total = row_max + jnp.log(jnp.sum(jnp.exp(scores - row_max), axis=-1, keepdims=True))
    probs_half = jnp.exp(scores - log_total).astype(jnp.bfloat16)
    heads_out = (
        product("shqk,skhe->sqhe", probs_half, proj_qkv[:, :, 2])
        .astype(jnp.bfloat16)
        .reshape(row_count, D)
    )
    resid_mid = resid_in + jnp.dot(heads_out, w_proj, preferred_element_type=jnp.float32)
    normed_two = normalize(resid_mid, gain_full[1], bias_full[1]).astype(jnp.bfloat16)
    pre_act = jnp.dot(normed_two, w_first, preferred_element_type=jnp.float32)
    activated = jax.nn.gelu(pre_act, approximate=False).astype(jnp.bfloat16)
    resid_out = resid_mid + jnp.dot(activated, w_second, preferred_element_type=jnp.float32)
    return (
        resid_out,
        (
            resid_in,
            normed_one,
            proj_qkv,
            heads_out,
            log_total,
            resid_mid,
            normed_two,
            pre_act,
            activated,
        ),
    )


def backward_layer(grad_stream, kept_acts, allowed, whole_set):
    gain, bias, w_query, w_proj, w_first, w_second = whole_set
    (
        resid_in,
        normed_one,
        proj_qkv,
        heads_out,
        log_total,
        resid_mid,
        normed_two,
        pre_act,
        activated,
    ) = kept_acts
    row_count = grad_stream.shape[0]
    seq_count = row_count // SEQ
    gain_full = gain.astype(jnp.float32)
    bias_full = bias.astype(jnp.float32)
    grad_half = grad_stream.astype(jnp.bfloat16)
    grad_second = cross_rows(activated, grad_half)
    d_activated = against(grad_half, w_second)
    d_preact = jax.vjp(lambda inner_val: jax.nn.gelu(inner_val, approximate=False), pre_act)[1](
        d_activated
    )[0]
    d_preact = d_preact.astype(jnp.bfloat16)
    grad_first = cross_rows(normed_two, d_preact)
    d_normed_two = against(d_preact, w_first)
    pullback = jax.vjp(normalize, resid_mid, gain_full[1], bias_full[1])[1]
    d_mid_norm, d_gain_two, d_bias_two = pullback(d_normed_two)
    d_mid = grad_stream + d_mid_norm
    d_mid_half = d_mid.astype(jnp.bfloat16)
    grad_proj = cross_rows(heads_out, d_mid_half)
    d_heads = (
        against(d_mid_half, w_proj).astype(jnp.bfloat16).reshape(seq_count, SEQ, HEADS, HEAD_DIM)
    )
    query_part = proj_qkv[:, :, 0]
    key_part = proj_qkv[:, :, 1]
    value_part = proj_qkv[:, :, 2]
    scores = scores_of(query_part, key_part, allowed)
    probs_full = jnp.exp(scores - log_total)
    probs_half = probs_full.astype(jnp.bfloat16)
    d_value = product("shqk,sqhe->skhe", probs_half, d_heads)
    d_probs = product("sqhe,skhe->shqk", d_heads, value_part)
    heads_four = heads_out.reshape(seq_count, SEQ, HEADS, HEAD_DIM)
    row_delta = jnp.sum(d_heads.astype(jnp.float32) * heads_four.astype(jnp.float32), axis=-1)
    row_delta = jnp.transpose(row_delta, (0, 2, 1))[..., None]
    d_scores = (probs_full * (d_probs - row_delta) * 0.125).astype(jnp.bfloat16)
    d_query = product("shqk,skhe->sqhe", d_scores, key_part)
    d_key = product("shqk,sqhe->skhe", d_scores, query_part)
    d_qkv = (
        jnp.stack([d_query, d_key, d_value], axis=2).reshape(row_count, 3 * D).astype(jnp.bfloat16)
    )
    grad_query = cross_rows(normed_one, d_qkv)
    d_normed_one = against(d_qkv, w_query)
    pullback = jax.vjp(normalize, resid_in, gain_full[0], bias_full[0])[1]
    d_in_norm, d_gain_one, d_bias_one = pullback(d_normed_one)
    d_input = d_mid + d_in_norm
    grad_terms = (
        jnp.stack([d_gain_one, d_gain_two]),
        jnp.stack([d_bias_one, d_bias_two]),
        grad_query,
        grad_proj,
        grad_first,
        grad_second,
    )
    return (d_input, grad_terms)


def body(tokens, segments, ln_gain, ln_bias, w_qkv, w_out, w_fc1, w_fc2, cotangent):
    row_count = tokens.shape[0]
    allowed = allowed_mask(segments.reshape(row_count // SEQ, SEQ))
    stream = tokens.astype(jnp.float32)
    layer_idx = 0
    whole_set = (
        lax.all_gather(ln_gain[layer_idx], "fsdp", axis=1, tiled=True),
        lax.all_gather(ln_bias[layer_idx], "fsdp", axis=1, tiled=True),
        lax.all_gather(w_qkv[layer_idx], "fsdp", axis=0, tiled=True),
        lax.all_gather(w_out[layer_idx], "fsdp", axis=0, tiled=True),
        lax.all_gather(w_fc1[layer_idx], "fsdp", axis=0, tiled=True),
        lax.all_gather(w_fc2[layer_idx], "fsdp", axis=0, tiled=True),
    )
    stream, kept_acts = forward_layer(stream, allowed, whole_set)
    stored = [kept_acts]
    fetched = [whole_set]
    block_output = stream.astype(jnp.bfloat16)
    grad_stream = cotangent.astype(jnp.float32)
    shares = [None] * LAYERS
    for layer_idx in reversed(range(LAYERS)):
        whole_set = fetched[layer_idx]
        grad_stream, grad_terms = backward_layer(grad_stream, stored[layer_idx], allowed, whole_set)
        summed_part = (
            lax.psum_scatter(
                grad_terms[0].astype(jnp.bfloat16), "fsdp", scatter_dimension=1, tiled=True
            ).astype(jnp.float32),
            lax.psum_scatter(
                grad_terms[1].astype(jnp.bfloat16), "fsdp", scatter_dimension=1, tiled=True
            ).astype(jnp.float32),
            lax.psum_scatter(
                grad_terms[2].astype(jnp.bfloat16), "fsdp", scatter_dimension=0, tiled=True
            ).astype(jnp.float32),
            lax.psum_scatter(
                grad_terms[3].astype(jnp.bfloat16), "fsdp", scatter_dimension=0, tiled=True
            ).astype(jnp.float32),
            lax.psum_scatter(
                grad_terms[4].astype(jnp.bfloat16), "fsdp", scatter_dimension=0, tiled=True
            ).astype(jnp.float32),
            lax.psum_scatter(
                grad_terms[5].astype(jnp.bfloat16), "fsdp", scatter_dimension=0, tiled=True
            ).astype(jnp.float32),
        )
        column_sums = (
            lax.psum_scatter(
                summed_part[2].astype(jnp.bfloat16), "rep", scatter_dimension=1, tiled=True
            ).astype(jnp.float32),
            lax.psum_scatter(
                summed_part[3].astype(jnp.bfloat16), "rep", scatter_dimension=1, tiled=True
            ).astype(jnp.float32),
            lax.psum_scatter(
                summed_part[4].astype(jnp.bfloat16), "rep", scatter_dimension=1, tiled=True
            ).astype(jnp.float32),
            lax.psum_scatter(
                summed_part[5].astype(jnp.bfloat16), "rep", scatter_dimension=1, tiled=True
            ).astype(jnp.float32),
        )
        joined = (
            lax.all_gather(column_sums[0].astype(jnp.bfloat16), "rep", axis=1, tiled=True).astype(
                jnp.float32
            ),
            lax.all_gather(column_sums[1].astype(jnp.bfloat16), "rep", axis=1, tiled=True).astype(
                jnp.float32
            ),
            lax.all_gather(column_sums[2].astype(jnp.bfloat16), "rep", axis=1, tiled=True).astype(
                jnp.float32
            ),
            lax.all_gather(column_sums[3].astype(jnp.bfloat16), "rep", axis=1, tiled=True).astype(
                jnp.float32
            ),
        )
        norm_terms = lax.psum((summed_part[0], summed_part[1]), "rep")
        summed_part = (norm_terms[0], norm_terms[1], joined[0], joined[1], joined[2], joined[3])
        shares[layer_idx] = summed_part
    stacked = tuple((jnp.stack([shares[0][member]]) for member in range(6)))
    return (
        block_output,
        grad_stream,
        stacked[0],
        stacked[1],
        stacked[2],
        stacked[3],
        stacked[4],
        stacked[5],
    )


def solution(mesh):
    in_specs = (
        P(("rep", "fsdp"), None),
        P(("rep", "fsdp")),
        P(None, None, "fsdp"),
        P(None, None, "fsdp"),
        P(None, "fsdp", None),
        P(None, "fsdp", None),
        P(None, "fsdp", None),
        P(None, "fsdp", None),
        P(("rep", "fsdp"), None),
    )
    out_specs = (
        P(("rep", "fsdp"), None),
        P(("rep", "fsdp"), None),
        P(None, None, "fsdp"),
        P(None, None, "fsdp"),
        P(None, "fsdp", None),
        P(None, "fsdp", None),
        P(None, "fsdp", None),
        P(None, "fsdp", None),
    )
    return jax.shard_map(body, mesh=mesh, in_specs=in_specs, out_specs=out_specs, check_vma=False)
```

profile of v0, /device:TPU:1, one launch (start us, length us, event | category | flops | bytes accessed | tf_op | source)
XLA Modules:
  0.0 1419.2 jit_solution(9998316927995709905)
XLA Ops:
  14.3 83.0 %all-gather.1 = bf16[1,2,1088]{1,0,2:T(2,128)(2,1)S(1)} all-gather(bf16[1,2,34]{1,0,2:T(2,128)(2,1)S(1)} %copy.52), channel_id=3, replica_groups=mesh['rep'=4,'fsdp'=32] {'fsdp'}, dimensions={2}, use_global_device_ids=true | all-gather | bytes 4488 | tf_op jit(solution)/shard_map/all_gather | solution.py:162
  98.0 74.4 %all-gather = bf16[1,2,1088]{1,0,2:T(2,128)(2,1)S(1)} all-gather(bf16[1,2,34]{1,0,2:T(2,128)(2,1)S(1)} %copy.51), channel_id=2, replica_groups=mesh['rep'=4,'fsdp'=32] {'fsdp'}, dimensions={2}, use_global_device_ids=true | all-gather | bytes 4488 | tf_op jit(solution)/shard_map/all_gather | solution.py:161
  173.4 17.8 %slice_reduce_fusion = (f32[1088]{0:T(1024)S(1)}, f32[1088]{0:T(1024)S(1)}) fusion(f32[1,2,1088]{1,0,2:T(1,128)S(1)} %convert_element_type.146), kind=kLoop, calls=%fused_computation.79 | loop fusion | bytes 17408 | tf_op jit(solution)/shard_map/slice | solution.py:68
  191.3 18.0 %slice_reduce_fusion.1 = (f32[1088]{0:T(1024)S(1)}, f32[1088]{0:T(1024)S(1)}) fusion(f32[1,2,1088]{1,0,2:T(1,128)S(1)} %convert_element_type.145), kind=kLoop, calls=%fused_computation.80 | loop fusion | bytes 17408 | tf_op jit(solution)/shard_map/slice | solution.py:68
  209.3 8.4 fusion.15
  218.7 119.9 %all-gather.17.cloned.1.call-done = bf16[1,1088,1088]{2,0,1:T(2,128)(2,1)} async-done(((bf16[1,34,1088]{2,0,1:T(2,128)(2,1)}), bf16[1,1088,1088]{2,0,1:T(2,128)(2,1)}) %all-gather.17.cloned.1.call-update) | async-done | bytes 2367504 | tf_op jit(solution)/shard_map/all_gather | solution.py:164
  342.3 231.8 %all-gather.19.cloned.1.call-done = bf16[1,1088,4352]{2,0,1:T(2,128)(2,1)} async-done(((bf16[1,34,4352]{2,0,1:T(2,128)(2,1)}), bf16[1,1088,4352]{2,0,1:T(2,128)(2,1)}) %all-gather.19.cloned.1.call-update) | async-done | bytes 9469968 | tf_op jit(solution)/shard_map/all_gather | solution.py:165
  574.1 15.5 %multiply_convert_fusion = (bf16[128,4352]{1,0:T(8,128)(2,1)S(1)}, f32[128,4352]{1,0:T(8,128)}) fusion(bf16[1,1088,4352]{2,0,1:T(2,128)(2,1)} %all-gather.19.cloned.1.call-done, f32[128,1088]{0,1:T(8,128)S(1)} %get-tuple-element.60, f32[1088]{0:T(1024)S(1)} %get-tuple-element.41, f32[1088]{0:T(1024)S(1)} %get-tuple-element.39, f32[128]{0:T(128)S(1)} %fusion.74, ...), kind=kOutput, calls=%fused_computation.31 | convolution fusion | flops 1249058816 | bytes 13379072 | tf_op jit(solution)/shard_map/dot_general | solution.py:69
  589.6 5.3 convolution_convert_fusion
  598.1 124.8 %all-gather.21.cloned.1.call-done = bf16[1,4352,1088]{2,1,0:T(8,128)(2,1)} async-done(((bf16[1,136,1088]{2,1,0:T(8,128)(2,1)}), bf16[1,4352,1088]{2,1,0:T(8,128)(2,1)}) %all-gather.21.cloned.1.call-update) | async-done | bytes 9469968 | tf_op jit(solution)/shard_map/all_gather | solution.py:166
  722.9 9.4 add_convert_fusion
  732.3 9.1 multiply_reduce_fusion
  745.9 5.1 convolution_convert_fusion.2
  751.0 5.7 convolution_convert_fusion.1
  756.7 347.1 %fusion.78 = (bf16[40,3264]{1,0:T(8,128)(2,1)}, bf16[48,1088]{1,0:T(8,128)(2,1)S(1)}, bf16[40,4352]{1,0:T(8,128)(2,1)}) fusion(bf16[1088,3264]{1,0:T(8,128)(2,1)} %convolution_convert_fusion.2, bf16[1088,1088]{1,0:T(8,128)(2,1)S(1)} %convolution_convert_fusion.3, bf16[1088,4352]{1,0:T(8,128)(2,1)} %convolution_convert_fusion.1), kind=kCustom, calls=%all-reduce-scatter.3 | all-reduce-scatter fusion | flops 11419650 | bytes 19654144
  1106.4 6.0 collective-permute-start.11
  1112.5 3.8 collective-permute-start.10
  1116.4 7.5 fusion.77
  1133.5 9.0 collective-permute-start.7
  1143.8 66.8 %all-reduce.10 = (bf16[2,1088]{1,0:T(2,128)(2,1)S(1)}, bf16[2,1088]{1,0:T(2,128)(2,1)S(1)}) all-reduce(bf16[2,1088]{1,0:T(2,128)(2,1)S(1)} %pad_maximum_fusion.1, bf16[2,1088]{1,0:T(2,128)(2,1)S(1)} %pad_maximum_fusion.2), channel_id=8, replica_groups=mesh['rep'=4,'fsdp'=32] {'fsdp'}, use_global_device_ids=true, to_apply=%region_13.14.clone | all-reduce | flops 4352 | bytes 17408
  1222.9 34.0 %all-reduce.9 = (f32[1,2,34]{2,1,0:T(2,128)}, f32[1,2,34]{2,1,0:T(2,128)}) all-reduce(f32[1,2,34]{2,1,0:T(2,128)S(1)} %get-tuple-element.65, f32[1,2,34]{2,1,0:T(2,128)S(1)} %get-tuple-element.66), channel_id=1, replica_groups=mesh['rep'=4,'fsdp'=32] {'rep'}, use_global_device_ids=true, to_apply=%region_14.15 | all-reduce | flops 136 | bytes 1088 | tf_op jit(solution)/shard_map/psum | solution.py:225
  1259.6 8.8 concatenate.1
  1278.7 9.8 collective-permute-start.19
  1288.5 11.0 concatenate
  1302.6 23.2 %concatenate.2 = bf16[226,4352]{1,0:T(8,128)(2,1)} concatenate(bf16[26,4352]{1,0:T(8,128)(2,1)} %collective-permute-done.19, bf16[40,4352]{1,0:T(8,128)(2,1)} %collective-permute-done.18, bf16[40,4352]{1,0:T(8,128)(2,1)} %collective-permute-done.17, bf16[40,4352]{1,0:T(8,128)(2,1)} %collective-permute-done.16, bf16[40,4352]{1,0:T(8,128)(2,1)} %collective-permute-done.15, ...), dimensions={0} | concatenate | bytes 3934208
  1328.8 7.5 fusion.28
  1340.5 9.4 all-gather.7
  1352.0 7.8 all-gather.6
  1361.4 8.7 reduce-scatter.29.cloned.1.call-done
  1371.2 8.3 all-gather.8
  1381.5 20.0 %reduce-scatter.31.cloned.1.call-done = bf16[272,136]{1,0:T(8,128)(2,1)} async-done(((bf16[1088,136]{1,0:T(8,128)(2,1)}), bf16[272,136]{1,0:T(8,128)(2,1)}) %reduce-scatter.31.cloned.1.call-update) | async-done | bytes 74000
  1402.5 8.4 all-gather.9
  (184 shorter events, 76.9 us)
Async XLA Ops:
  7.2 202.2 %all-gather.15.cloned.1.call-start = ((), (), s32[]{:S(2)}) async-start(), calls=%async_computation.5 | async-start | bytes 14936064 | tf_op jit(solution)/shard_map/all_gather | solution.py:163
  9.3 329.3 %all-gather.17.cloned.1.call-start = ((), (), s32[]{:S(2)}) async-start(), calls=%async_computation.6 | async-start | bytes 5170176 | tf_op jit(solution)/shard_map/all_gather | solution.py:164
  11.1 563.0 %all-gather.19.cloned.1.call-start = ((), (), s32[]{:S(2)}) async-start(), calls=%async_computation.7 | async-start | bytes 19531776 | tf_op jit(solution)/shard_map/all_gather | solution.py:165
  13.4 159.6 %copy-start = (bf16[128,1088]{0,1:T(8,128)(2,1)S(1)}, bf16[128,1088]{0,1:T(8,128)(2,1)}, u32[]{:S(2)}) copy-start(bf16[128,1088]{0,1:T(8,128)(2,1)} %param.9) | copy-start | bytes 835588
  13.4 159.9 %copy-start.22 = (s32[128]{0:T(128)S(1)}, s32[128]{0:T(128)}, u32[]{:S(2)}) copy-start(s32[128]{0:T(128)} %param.10) | copy-start | bytes 1540
  13.4 709.5 %all-gather.21.cloned.1.call-start = ((), (), s32[]{:S(2)}) async-start(), calls=%async_computation.8 | async-start | bytes 10340352 | tf_op jit(solution)/shard_map/all_gather | solution.py:166
  14.0 1322.4 %reduce-scatter.33.cloned.1.call-start = ((), (), s32[]{:S(2)}) async-start(), calls=%async_computation.13 | async-start | bytes 10340352
  218.7 123.6 %copy-start.9 = (bf16[17,64,128]{2,1,0:T(8,128)(2,1)}, bf16[17,64,128]{2,1,0:T(8,128)(2,1)S(1)}, u32[]{:S(2)}) copy-start(bf16[17,64,128]{2,1,0:T(8,128)(2,1)S(1)} %convolution_convert_fusion.7) | copy-start | bytes 835588
  595.0 744.5 %reduce-scatter.27.cloned.1.call-start = ((), (), s32[]{:S(2)}) async-start(), calls=%async_computation.10 | async-start | bytes 348160
  1103.8 27.1 %collective-permute-start.13 = (bf16[48,1088]{1,0:T(8,128)(2,1)S(1)}, bf16[48,1088]{1,0:T(8,128)(2,1)S(1)}, u32[]{:S(2)}, u32[]{:S(2)}) collective-permute-start(bf16[48,1088]{1,0:T(8,128)(2,1)S(1)} %get-tuple-element.51), channel_id=1, source_target_pairs={{0,9},{1,10},{2,11},{3,12},{4,13},{5,14},{6,15},{7,16},{8,17},{9,1... | collective-permute-start | bytes 313352
  1105.1 28.4 %collective-permute-start.12 = (bf16[48,1088]{1,0:T(8,128)(2,1)S(1)}, bf16[48,1088]{1,0:T(8,128)(2,1)S(1)}, u32[]{:S(2)}, u32[]{:S(2)}) collective-permute-start(bf16[48,1088]{1,0:T(8,128)(2,1)S(1)} %get-tuple-element.51), channel_id=1, source_target_pairs={{0,8},{1,9},{2,10},{3,11},{4,12},{5,13},{6,14},{7,15},{8,16},{9,17... | collective-permute-start | bytes 313352
  1106.4 36.1 %collective-permute-start.11 = (bf16[48,1088]{1,0:T(8,128)(2,1)S(1)}, bf16[48,1088]{1,0:T(8,128)(2,1)S(1)}, u32[]{:S(2)}, u32[]{:S(2)}) collective-permute-start(bf16[48,1088]{1,0:T(8,128)(2,1)S(1)} %get-tuple-element.51), channel_id=1, source_target_pairs={{0,7},{1,8},{2,9},{3,10},{4,11},{5,12},{6,13},{7,14},{8,15},{9,16}... | collective-permute-start | bytes 313352
  1112.5 98.2 %collective-permute-start.10 = (bf16[48,1088]{1,0:T(8,128)(2,1)S(1)}, bf16[48,1088]{1,0:T(8,128)(2,1)S(1)}, u32[]{:S(2)}, u32[]{:S(2)}) collective-permute-start(bf16[48,1088]{1,0:T(8,128)(2,1)S(1)} %get-tuple-element.51), channel_id=1, source_target_pairs={{0,6},{1,7},{2,8},{3,9},{4,10},{5,11},{6,12},{7,13},{8,14},{9,15},... | collective-permute-start | bytes 313352
  1124.3 2.9 collective-permute-start.14
  1127.2 85.5 %collective-permute-start.9 = (bf16[48,1088]{1,0:T(8,128)(2,1)S(1)}, bf16[48,1088]{1,0:T(8,128)(2,1)S(1)}, u32[]{:S(2)}, u32[]{:S(2)}) collective-permute-start(bf16[48,1088]{1,0:T(8,128)(2,1)S(1)} %get-tuple-element.51), channel_id=1, source_target_pairs={{0,5},{1,6},{2,7},{3,8},{4,9},{5,10},{6,11},{7,12},{8,13},{9,14},{... | collective-permute-start | bytes 313352
  1130.9 83.8 %collective-permute-start.8 = (bf16[48,1088]{1,0:T(8,128)(2,1)S(1)}, bf16[48,1088]{1,0:T(8,128)(2,1)S(1)}, u32[]{:S(2)}, u32[]{:S(2)}) collective-permute-start(bf16[48,1088]{1,0:T(8,128)(2,1)S(1)} %get-tuple-element.51), channel_id=1, source_target_pairs={{0,4},{1,5},{2,6},{3,7},{4,8},{5,9},{6,10},{7,11},{8,12},{9,13},{1... | collective-permute-start | bytes 313352
  1133.5 83.2 %collective-permute-start.7 = (bf16[48,1088]{1,0:T(8,128)(2,1)S(1)}, bf16[48,1088]{1,0:T(8,128)(2,1)S(1)}, u32[]{:S(2)}, u32[]{:S(2)}) collective-permute-start(bf16[48,1088]{1,0:T(8,128)(2,1)S(1)} %get-tuple-element.51), channel_id=1, source_target_pairs={{0,3},{1,4},{2,5},{3,6},{4,7},{5,8},{6,9},{7,10},{8,11},{9,12},{10... | collective-permute-start | bytes 313352
  1142.5 76.2 %collective-permute-start.6 = (bf16[48,1088]{1,0:T(8,128)(2,1)S(1)}, bf16[48,1088]{1,0:T(8,128)(2,1)S(1)}, u32[]{:S(2)}, u32[]{:S(2)}) collective-permute-start(bf16[48,1088]{1,0:T(8,128)(2,1)S(1)} %get-tuple-element.51), channel_id=1, source_target_pairs={{0,2},{1,3},{2,4},{3,5},{4,6},{5,7},{6,8},{7,9},{8,10},{9,11},{10,... | collective-permute-start | bytes 313352
  1210.7 46.2 %collective-permute-start.5 = (bf16[48,1088]{1,0:T(8,128)(2,1)S(1)}, bf16[48,1088]{1,0:T(8,128)(2,1)S(1)}, u32[]{:S(2)}, u32[]{:S(2)}) collective-permute-start(bf16[48,1088]{1,0:T(8,128)(2,1)S(1)} %get-tuple-element.51), channel_id=1, source_target_pairs={{0,1},{1,2},{2,3},{3,4},{4,5},{5,6},{6,7},{7,8},{8,9},{9,10},{10,1... | collective-permute-start | bytes 313352
  1212.7 58.8 %collective-permute-start.3 = (bf16[40,3264]{1,0:T(8,128)(2,1)S(1)}, bf16[40,3264]{1,0:T(8,128)(2,1)}, u32[]{:S(2)}, u32[]{:S(2)}) collective-permute-start(bf16[40,3264]{1,0:T(8,128)(2,1)S(1)} %copy-done.11), channel_id=1, source_target_pairs={{0,4},{1,5},{2,6},{3,7},{4,8},{5,9},{6,10},{7,11},{8,12},{9,13},{1... | collective-permute-start | bytes 783368
  1214.7 58.9 %collective-permute-start.2 = (bf16[40,3264]{1,0:T(8,128)(2,1)S(1)}, bf16[40,3264]{1,0:T(8,128)(2,1)}, u32[]{:S(2)}, u32[]{:S(2)}) collective-permute-start(bf16[40,3264]{1,0:T(8,128)(2,1)S(1)} %copy-done.11), channel_id=1, source_target_pairs={{0,3},{1,4},{2,5},{3,6},{4,7},{5,8},{6,9},{7,10},{8,11},{9,12},{10... | collective-permute-start | bytes 783368
  1216.7 59.2 %collective-permute-start.1 = (bf16[40,3264]{1,0:T(8,128)(2,1)S(1)}, bf16[40,3264]{1,0:T(8,128)(2,1)}, u32[]{:S(2)}, u32[]{:S(2)}) collective-permute-start(bf16[40,3264]{1,0:T(8,128)(2,1)S(1)} %copy-done.11), channel_id=1, source_target_pairs={{0,2},{1,3},{2,4},{3,5},{4,6},{5,7},{6,8},{7,9},{8,10},{9,11},{10,... | collective-permute-start | bytes 783368
  1218.7 60.0 %collective-permute-start = (bf16[40,3264]{1,0:T(8,128)(2,1)S(1)}, bf16[40,3264]{1,0:T(8,128)(2,1)}, u32[]{:S(2)}, u32[]{:S(2)}) collective-permute-start(bf16[40,3264]{1,0:T(8,128)(2,1)S(1)} %copy-done.11), channel_id=1, source_target_pairs={{0,1},{1,2},{2,3},{3,4},{4,5},{5,6},{6,7},{7,8},{8,9},{9,10},{10,1... | collective-permute-start | bytes 783368
  1257.6 11.8 collective-permute-start.4
  1269.3 81.6 %reduce-scatter.25.cloned.1.call-start = ((), (), s32[]{:S(2)}) async-start(), calls=%async_computation.9 | async-start | bytes 1044480
  1269.4 33.2 %collective-permute-start.18 = (bf16[40,4352]{1,0:T(8,128)(2,1)S(1)}, bf16[40,4352]{1,0:T(8,128)(2,1)}, u32[]{:S(2)}, u32[]{:S(2)}) collective-permute-start(bf16[40,4352]{1,0:T(8,128)(2,1)S(1)} %copy-done.6), channel_id=1, source_target_pairs={{0,4},{1,5},{2,6},{3,7},{4,8},{5,9},{6,10},{7,11},{8,12},{9,13},{1... | collective-permute-start | bytes 1044488
  1271.4 31.2 %collective-permute-start.17 = (bf16[40,4352]{1,0:T(8,128)(2,1)S(1)}, bf16[40,4352]{1,0:T(8,128)(2,1)}, u32[]{:S(2)}, u32[]{:S(2)}) collective-permute-start(bf16[40,4352]{1,0:T(8,128)(2,1)S(1)} %copy-done.6), channel_id=1, source_target_pairs={{0,3},{1,4},{2,5},{3,6},{4,7},{5,8},{6,9},{7,10},{8,11},{9,12},{10... | collective-permute-start | bytes 1044488
  1273.6 29.0 %collective-permute-start.16 = (bf16[40,4352]{1,0:T(8,128)(2,1)S(1)}, bf16[40,4352]{1,0:T(8,128)(2,1)}, u32[]{:S(2)}, u32[]{:S(2)}) collective-permute-start(bf16[40,4352]{1,0:T(8,128)(2,1)S(1)} %copy-done.6), channel_id=1, source_target_pairs={{0,2},{1,3},{2,4},{3,5},{4,6},{5,7},{6,8},{7,9},{8,10},{9,11},{10,... | collective-permute-start | bytes 1044488
  1275.9 26.7 %collective-permute-start.15 = (bf16[40,4352]{1,0:T(8,128)(2,1)S(1)}, bf16[40,4352]{1,0:T(8,128)(2,1)}, u32[]{:S(2)}, u32[]{:S(2)}) collective-permute-start(bf16[40,4352]{1,0:T(8,128)(2,1)S(1)} %copy-done.6), channel_id=1, source_target_pairs={{0,1},{1,2},{2,3},{3,4},{4,5},{5,6},{6,7},{7,8},{8,9},{9,10},{10,1... | collective-permute-start | bytes 1044488
  1278.7 23.8 %collective-permute-start.19 = (bf16[26,4352]{1,0:T(8,128)(2,1)}, bf16[26,4352]{1,0:T(8,128)(2,1)}, u32[]{:S(2)}, u32[]{:S(2)}) collective-permute-start(bf16[26,4352]{1,0:T(8,128)(2,1)} %slice.46), channel_id=1, source_target_pairs={{0,5},{1,6},{2,7},{3,8},{4,9},{5,10},{6,11},{7,12},{8,13},{9,14},{... | collective-permute-start | bytes 678920
  1302.5 67.6 %reduce-scatter.29.cloned.1.call-start = ((), (), s32[]{:S(2)}) async-start(), calls=%async_computation.11 | async-start | bytes 1392640
  1328.5 73.0 %reduce-scatter.31.cloned.1.call-start = ((), (), s32[]{:S(2)}) async-start(), calls=%async_computation.12 | async-start | bytes 696320
  (25 other events, 752.7 us)
Sparse Core Ops, SparseCore 0:
  10.2 174.8 all-gather.14
  187.3 151.2 all-gather.16
  340.8 233.2 all-gather.18
  575.6 147.2 all-gather.20
  725.2 233.5 reduce-scatter.32
  1269.5 31.2 reduce-scatter.26
  1303.4 32.4 reduce-scatter.24
  1338.5 31.5 reduce-scatter.28
  1373.3 28.1 reduce-scatter.30
where the time goes:
time: 1430 us; the launch traced here: 1420 us
  blocking collectives  639 us (45%)
  waiting for transfers between devices  507 us (35%)
  local copies, waits for them, and re-layouts  108 us (8%)
  matrix products  81.1 us (6%)
  starting transfers between devices  63.5 us (4%)
  between operations  17 us (1%)
    unnamed x2, blocking collectives  414 us
    all_gather x1, waiting for transfers between devices, body(): lax.all_gather(w_fc1[layer_idx], 'fsdp', axis=0, tiled=True)  232 us
    all_gather x1, waiting for transfers between devices, body(): lax.all_gather(w_fc2[layer_idx], 'fsdp', axis=0, tiled=True)  125 us
    all_gather x1, waiting for transfers between devices, body(): lax.all_gather(w_out[layer_idx], 'fsdp', axis=0, tiled=True)  120 us
    all_gather x1, blocking collectives, body(): lax.all_gather(ln_bias[layer_idx], 'fsdp', axis=1, tiled=True)  83 us
    all_gather x1, blocking collectives, body(): lax.all_gather(ln_gain[layer_idx], 'fsdp', axis=1, tiled=True)  74.4 us
    unnamed x82, local copies, waits for them, and re-layouts  69.4 us
    unnamed x25, starting transfers between devices  63.3 us
  transfers between devices with their start and end apart: 29, of which 6 were waited for; matrix products, arithmetic and copies ran while one was open for 38% of the time, Pallas kernels for 0%

commit v1 on v0

--- a/solution.py
+++ b/solution.py
@@ -162,7 +162,10 @@
         lax.all_gather(ln_bias[layer_idx], "fsdp", axis=1, tiled=True),
         lax.all_gather(w_qkv[layer_idx], "fsdp", axis=0, tiled=True),
         lax.all_gather(w_out[layer_idx], "fsdp", axis=0, tiled=True),
-        lax.all_gather(w_fc1[layer_idx], "fsdp", axis=0, tiled=True),
+        jnp.concatenate(
+            lax.all_to_all(jnp.stack([w_fc1[layer_idx]] * lax.axis_size("fsdp")), "fsdp", 0, 0),
+            axis=0,
+        ),
         lax.all_gather(w_fc2[layer_idx], "fsdp", axis=0, tiled=True),
     )
     stream, kept_acts = forward_layer(stream, allowed, whole_set)

time: 1430 us -> 1360 us (0.951)
  waiting for transfers between devices: 507 us -> 203 us
  blocking collectives: 639 us -> 840 us
  local copies, waits for them, and re-layouts: 108 us -> 135 us
    all_gather x1 -> x0, waiting for transfers between devices: 232 us -> none  [body(): lax.all_gather(w_fc1[layer_idx], 'fsdp', axis=0, tiled=True)]
    all_gather x1, blocking collectives: 83 us -> 291 us  [body(): lax.all_gather(ln_bias[layer_idx], 'fsdp', axis=1, tiled=True)]
    all_gather x1, waiting for transfers between devices: 120 us -> 28.8 us  [body(): lax.all_gather(w_out[layer_idx], 'fsdp', axis=0, tiled=True)]
    all_gather x1, waiting for transfers between devices: 125 us -> 147 us  [body(): lax.all_gather(w_fc2[layer_idx], 'fsdp', axis=0, tiled=True)]
    unnamed x82 -> x81, local copies, waits for them, and re-layouts: 69.4 us -> 79.5 us
    unnamed x34 -> x33, waiting for transfers between devices: 30.1 us -> 27 us
  transfers between devices with their start and end apart: 29 -> 29, of which waited for: 6 -> 5; matrix products, arithmetic and copies ran while one was open for 38% -> 41% of each run, Pallas kernels for 0% -> 0%
where the time goes in v1:
time: 1360 us; the launch traced here: 1350 us
  blocking collectives  840 us (62%)
  waiting for transfers between devices  203 us (15%)
  local copies, waits for them, and re-layouts  135 us (10%)
  matrix products  78.8 us (6%)
  starting transfers between devices  71.7 us (5%)
  between operations  17.3 us (1%)
    unnamed x2, blocking collectives  412 us
    all_gather x1, blocking collectives, body(): lax.all_gather(ln_bias[layer_idx], 'fsdp', axis=1, tiled=True)  291 us
    all_gather x1, waiting for transfers between devices, body(): lax.all_gather(w_fc2[layer_idx], 'fsdp', axis=0, tiled=True)  147 us
    unnamed x81, local copies, waits for them, and re-layouts  79.5 us
    all_gather x1, blocking collectives, body(): lax.all_gather(ln_gain[layer_idx], 'fsdp', axis=1, tiled=True)  69 us
    unnamed x25, starting transfers between devices  61.6 us
    psum x1, blocking collectives, body(): norm_terms = lax.psum((summed_part[0], summed_part[1]), 'rep')  33.3 us
    all_gather x1, waiting for transfers between devices, body(): lax.all_gather(w_out[layer_idx], 'fsdp', axis=0, tiled=True)  28.8 us
  transfers between devices with their start and end apart: 29, of which 5 were waited for; matrix products, arithmetic and copies ran while one was open for 41% of the time, Pallas kernels for 0%

profile of v1, /device:TPU:1, one launch (start us, length us, event | category | flops | bytes accessed | tf_op | source)
XLA Modules:
  0.0 1351.0 jit_solution(3637587420638173629)
XLA Ops:
  11.8 5.8 stack.65
  17.6 10.0 all-to-all-start
  27.8 291.2 %all-gather.1 = bf16[1,2,1088]{1,0,2:T(2,128)(2,1)S(1)} all-gather(bf16[1,2,34]{1,0,2:T(2,128)(2,1)S(1)} %copy.51), channel_id=3, replica_groups=mesh['rep'=4,'fsdp'=32] {'fsdp'}, dimensions={2}, use_global_device_ids=true | all-gather | bytes 4488 | tf_op jit(solution)/shard_map/all_gather | solution.py:162
  319.7 69.0 %all-gather = bf16[1,2,1088]{1,0,2:T(2,128)(2,1)S(1)} all-gather(bf16[1,2,34]{1,0,2:T(2,128)(2,1)S(1)} %copy.50), channel_id=2, replica_groups=mesh['rep'=4,'fsdp'=32] {'fsdp'}, dimensions={2}, use_global_device_ids=true | all-gather | bytes 4488 | tf_op jit(solution)/shard_map/all_gather | solution.py:161
  389.8 17.8 %slice_reduce_fusion = (f32[1088]{0:T(1024)S(1)}, f32[1088]{0:T(1024)S(1)}) fusion(f32[1,2,1088]{1,0,2:T(1,128)S(1)} %convert_element_type.146), kind=kLoop, calls=%fused_computation.73 | loop fusion | bytes 17408 | tf_op jit(solution)/shard_map/slice | solution.py:68
  407.6 18.1 %slice_reduce_fusion.1 = (f32[1088]{0:T(1024)S(1)}, f32[1088]{0:T(1024)S(1)}) fusion(f32[1,2,1088]{1,0,2:T(1,128)S(1)} %convert_element_type.145), kind=kLoop, calls=%fused_computation.74 | loop fusion | bytes 17408 | tf_op jit(solution)/shard_map/slice | solution.py:68
  425.7 10.9 reshape.250
  436.6 8.4 fusion.11
  446.3 28.8 %all-gather.15.cloned.1.call-done = bf16[1,1088,1088]{2,0,1:T(2,128)(2,1)} async-done(((bf16[1,34,1088]{2,0,1:T(2,128)(2,1)}), bf16[1,1088,1088]{2,0,1:T(2,128)(2,1)}) %all-gather.15.cloned.1.call-update) | async-done | bytes 2367504 | tf_op jit(solution)/shard_map/all_gather | solution.py:164
  478.8 9.9 multiply_convert_fusion
  489.7 5.3 convolution_convert_fusion
  498.2 147.5 %all-gather.17.cloned.1.call-done = bf16[1,4352,1088]{2,1,0:T(8,128)(2,1)} async-done(((bf16[1,136,1088]{2,1,0:T(8,128)(2,1)}), bf16[1,4352,1088]{2,1,0:T(8,128)(2,1)}) %all-gather.17.cloned.1.call-update) | async-done | bytes 9469968 | tf_op jit(solution)/shard_map/all_gather | solution.py:169
  645.7 17.8 %add_convert_fusion = bf16[128,4352]{1,0:T(8,128)(2,1)S(1)} fusion(bf16[128,1088]{0,1:T(8,128)(2,1)S(1)} %copy-done.5, bf16[1,4352,1088]{2,1,0:T(8,128)(2,1)} %all-gather.17.cloned.1.call-done, f32[128,4352]{1,0:T(8,128)} %get-tuple-element.62), kind=kOutput, calls=%fused_computation.24 | convolution fusion | flops 1252261888 | bytes 13090816 | tf_op jit(solution)/shard_map/dot_general | solution.py:28
  672.2 5.1 convolution_convert_fusion.2
  677.4 5.4 convolution_convert_fusion.1
  682.8 346.1 %fusion.73 = (bf16[40,3264]{1,0:T(8,128)(2,1)S(1)}, bf16[48,1088]{1,0:T(8,128)(2,1)S(1)}, bf16[40,4352]{1,0:T(8,128)(2,1)S(1)}) fusion(bf16[1088,3264]{1,0:T(8,128)(2,1)} %convolution_convert_fusion.2, bf16[1088,1088]{1,0:T(8,128)(2,1)} %convolution_convert_fusion.3, bf16[1088,4352]{1,0:T(8,128)(2,1)} %convolution_convert_fusion.1), kind=kCustom, calls=%all-reduce-scatter.3 | all-reduce-scatter fusion | flops 11419650 | bytes 19654144
  1031.5 6.6 collective-permute-start.11
  1040.1 7.3 fusion.72
  1056.0 9.0 collective-permute-start.7
  1066.9 66.3 %all-reduce.10 = (bf16[2,1088]{1,0:T(2,128)(2,1)S(1)}, bf16[2,1088]{1,0:T(2,128)(2,1)S(1)}) all-reduce(bf16[2,1088]{1,0:T(2,128)(2,1)S(1)} %pad_maximum_fusion.1, bf16[2,1088]{1,0:T(2,128)(2,1)S(1)} %pad_maximum_fusion.2), channel_id=7, replica_groups=mesh['rep'=4,'fsdp'=32] {'fsdp'}, use_global_device_ids=true, to_apply=%region_13.14.clone | all-reduce | flops 4352 | bytes 17408
  1145.0 33.3 %all-reduce.9 = (f32[1,2,34]{2,1,0:T(2,128)}, f32[1,2,34]{2,1,0:T(2,128)}) all-reduce(f32[1,2,34]{2,1,0:T(2,128)S(1)} %get-tuple-element.65, f32[1,2,34]{2,1,0:T(2,128)S(1)} %get-tuple-element.66), channel_id=1, replica_groups=mesh['rep'=4,'fsdp'=32] {'rep'}, use_global_device_ids=true, to_apply=%region_14.15 | all-reduce | flops 136 | bytes 1088 | tf_op jit(solution)/shard_map/psum | solution.py:228
  1179.7 16.3 %concatenate.1 = bf16[482,1088]{1,0:T(8,128)(2,1)} concatenate(bf16[2,1088]{1,0:T(2,128)(2,1)S(1)} %collective-permute-done.14, bf16[48,1088]{1,0:T(8,128)(2,1)S(1)} %collective-permute-done.13, bf16[48,1088]{1,0:T(8,128)(2,1)S(1)} %collective-permute-done.12, bf16[48,1088]{1,0:T(8,128)(2,1)} %copy-done.11, bf16[48,1088]{1,0:T(8,128)(2,1)} %collective-permute-done.10, ...), dimensions={0} | concatenate | bytes 2097664
  1209.5 9.0 collective-permute-start.19
  1218.5 16.0 %concatenate = bf16[226,3264]{1,0:T(8,128)(2,1)} concatenate(bf16[26,3264]{1,0:T(8,128)(2,1)S(1)} %collective-permute-done.4, bf16[40,3264]{1,0:T(8,128)(2,1)S(1)} %collective-permute-done.3, bf16[40,3264]{1,0:T(8,128)(2,1)} %collective-permute-done.2, bf16[40,3264]{1,0:T(8,128)(2,1)} %collective-permute-done.1, bf16[40,3264]{1,0:T(8,128)(2,1)} %collective-permute-done, ...), dimensions={0} | concatenate | bytes 2950656
  1237.0 22.3 %concatenate.2 = bf16[226,4352]{1,0:T(8,128)(2,1)} concatenate(bf16[26,4352]{1,0:T(8,128)(2,1)} %collective-permute-done.19, bf16[40,4352]{1,0:T(8,128)(2,1)S(1)} %collective-permute-done.18, bf16[40,4352]{1,0:T(8,128)(2,1)S(1)} %collective-permute-done.17, bf16[40,4352]{1,0:T(8,128)(2,1)} %collective-permute-done.16, bf16[40,4352]{1,0:T(8,128)(2,1)} %collective-permute-done.15, ...), dimensions={0} | concatenate | bytes 3934208
  1262.0 7.6 fusion.22
  1274.8 9.7 all-gather.6
  1286.6 7.8 all-gather.5
  1296.1 5.5 reduce-scatter.29.cloned.1.call-done
  1302.7 8.3 all-gather.7
  1312.9 20.0 %reduce-scatter.31.cloned.1.call-done = bf16[272,136]{1,0:T(8,128)(2,1)} async-done(((bf16[1088,136]{1,0:T(8,128)(2,1)}), bf16[272,136]{1,0:T(8,128)(2,1)}) %reduce-scatter.31.cloned.1.call-update) | async-done | bytes 74000
  1333.9 8.4 all-gather.8
  (185 shorter events, 83.1 us)
Async XLA Ops:
  7.2 429.5 %all-gather.13.cloned.1.call-start = ((), (), s32[]{:S(2)}) async-start(), calls=%async_computation.6 | async-start | bytes 14936064 | tf_op jit(solution)/shard_map/all_gather | solution.py:163
  9.3 465.8 %all-gather.15.cloned.1.call-start = ((), (), s32[]{:S(2)}) async-start(), calls=%async_computation.7 | async-start | bytes 5170176 | tf_op jit(solution)/shard_map/all_gather | solution.py:164
  11.1 634.6 %all-gather.17.cloned.1.call-start = ((), (), s32[]{:S(2)}) async-start(), calls=%async_computation.8 | async-start | bytes 10340352 | tf_op jit(solution)/shard_map/all_gather | solution.py:169
  17.6 302.0 %copy-start.22 = (bf16[1,2,34]{2,1,0:T(2,128)(2,1)S(1)}, bf16[1,2,34]{2,1,0:T(2,128)(2,1)}, u32[]{:S(2)}) copy-start(bf16[1,2,34]{2,1,0:T(2,128)(2,1)} %param.11) | copy-start | bytes 412
  17.6 408.1 %all-to-all-start = ((bf16[32,34,4352]{2,1,0:T(8,128)(2,1)}), bf16[32,34,4352]{2,1,0:T(8,128)(2,1)}, u32[]{:S(2)}, u32[]{:S(2)}) async-start(bf16[32,34,4352]{2,1,0:T(8,128)(2,1)} %stack.65), calls=%async_computation | async-start | bytes 22282240 | tf_op jit(solution)/shard_map/all_to_all | solution.py:166
  27.6 361.8 %copy-start = (bf16[128,1088]{0,1:T(8,128)(2,1)S(1)}, bf16[128,1088]{0,1:T(8,128)(2,1)}, u32[]{:S(2)}) copy-start(bf16[128,1088]{0,1:T(8,128)(2,1)} %param.9) | copy-start | bytes 835588
  27.6 362.1 %copy-start.15 = (s32[128]{0:T(128)S(1)}, s32[128]{0:T(128)}, u32[]{:S(2)}) copy-start(s32[128]{0:T(128)} %param.10) | copy-start | bytes 1540
  27.6 1242.0 %reduce-scatter.33.cloned.1.call-start = ((), (), s32[]{:S(2)}) async-start(), calls=%async_computation.13 | async-start | bytes 10340352
  495.1 778.7 %reduce-scatter.27.cloned.1.call-start = ((), (), s32[]{:S(2)}) async-start(), calls=%async_computation.10 | async-start | bytes 348160
  1028.9 25.1 %collective-permute-start.13 = (bf16[48,1088]{1,0:T(8,128)(2,1)S(1)}, bf16[48,1088]{1,0:T(8,128)(2,1)S(1)}, u32[]{:S(2)}, u32[]{:S(2)}) collective-permute-start(bf16[48,1088]{1,0:T(8,128)(2,1)S(1)} %get-tuple-element.51), channel_id=1, source_target_pairs={{0,9},{1,10},{2,11},{3,12},{4,13},{5,14},{6,15},{7,16},{8,17},{9,1... | collective-permute-start | bytes 313352
  1030.2 25.7 %collective-permute-start.12 = (bf16[48,1088]{1,0:T(8,128)(2,1)S(1)}, bf16[48,1088]{1,0:T(8,128)(2,1)S(1)}, u32[]{:S(2)}, u32[]{:S(2)}) collective-permute-start(bf16[48,1088]{1,0:T(8,128)(2,1)S(1)} %get-tuple-element.51), channel_id=1, source_target_pairs={{0,8},{1,9},{2,10},{3,11},{4,12},{5,13},{6,14},{7,15},{8,16},{9,17... | collective-permute-start | bytes 313352
  1031.5 33.5 %collective-permute-start.11 = (bf16[48,1088]{1,0:T(8,128)(2,1)S(1)}, bf16[48,1088]{1,0:T(8,128)(2,1)S(1)}, u32[]{:S(2)}, u32[]{:S(2)}) collective-permute-start(bf16[48,1088]{1,0:T(8,128)(2,1)S(1)} %get-tuple-element.51), channel_id=1, source_target_pairs={{0,7},{1,8},{2,9},{3,10},{4,11},{5,12},{6,13},{7,14},{8,15},{9,16}... | collective-permute-start | bytes 313352
  1038.2 95.1 %collective-permute-start.10 = (bf16[48,1088]{1,0:T(8,128)(2,1)S(1)}, bf16[48,1088]{1,0:T(8,128)(2,1)}, u32[]{:S(2)}, u32[]{:S(2)}) collective-permute-start(bf16[48,1088]{1,0:T(8,128)(2,1)S(1)} %get-tuple-element.51), channel_id=1, source_target_pairs={{0,6},{1,7},{2,8},{3,9},{4,10},{5,11},{6,12},{7,13},{8,14},{9,15},... | collective-permute-start | bytes 313352
  1047.9 2.0 collective-permute-start.14
  1049.9 84.7 %collective-permute-start.9 = (bf16[48,1088]{1,0:T(8,128)(2,1)S(1)}, bf16[48,1088]{1,0:T(8,128)(2,1)S(1)}, u32[]{:S(2)}, u32[]{:S(2)}) collective-permute-start(bf16[48,1088]{1,0:T(8,128)(2,1)S(1)} %get-tuple-element.51), channel_id=1, source_target_pairs={{0,5},{1,6},{2,7},{3,8},{4,9},{5,10},{6,11},{7,12},{8,13},{9,14},{... | collective-permute-start | bytes 313352
  1054.0 82.6 %collective-permute-start.8 = (bf16[48,1088]{1,0:T(8,128)(2,1)S(1)}, bf16[48,1088]{1,0:T(8,128)(2,1)S(1)}, u32[]{:S(2)}, u32[]{:S(2)}) collective-permute-start(bf16[48,1088]{1,0:T(8,128)(2,1)S(1)} %get-tuple-element.51), channel_id=1, source_target_pairs={{0,4},{1,5},{2,6},{3,7},{4,8},{5,9},{6,10},{7,11},{8,12},{9,13},{1... | collective-permute-start | bytes 313352
  1056.0 82.6 %collective-permute-start.7 = (bf16[48,1088]{1,0:T(8,128)(2,1)S(1)}, bf16[48,1088]{1,0:T(8,128)(2,1)S(1)}, u32[]{:S(2)}, u32[]{:S(2)}) collective-permute-start(bf16[48,1088]{1,0:T(8,128)(2,1)S(1)} %get-tuple-element.51), channel_id=1, source_target_pairs={{0,3},{1,4},{2,5},{3,6},{4,7},{5,8},{6,9},{7,10},{8,11},{9,12},{10... | collective-permute-start | bytes 313352
  1065.6 76.5 %collective-permute-start.6 = (bf16[48,1088]{1,0:T(8,128)(2,1)S(1)}, bf16[48,1088]{1,0:T(8,128)(2,1)S(1)}, u32[]{:S(2)}, u32[]{:S(2)}) collective-permute-start(bf16[48,1088]{1,0:T(8,128)(2,1)S(1)} %get-tuple-element.51), channel_id=1, source_target_pairs={{0,2},{1,3},{2,4},{3,5},{4,6},{5,7},{6,8},{7,9},{8,10},{9,11},{10,... | collective-permute-start | bytes 313352
  1133.3 66.0 %collective-permute-start.3 = (bf16[40,3264]{1,0:T(8,128)(2,1)S(1)}, bf16[40,3264]{1,0:T(8,128)(2,1)S(1)}, u32[]{:S(2)}, u32[]{:S(2)}) collective-permute-start(bf16[40,3264]{1,0:T(8,128)(2,1)S(1)} %get-tuple-element.50), channel_id=1, source_target_pairs={{0,4},{1,5},{2,6},{3,7},{4,8},{5,9},{6,10},{7,11},{8,12},{9,13},{1... | collective-permute-start | bytes 783368
  1134.6 66.9 %collective-permute-start.2 = (bf16[40,3264]{1,0:T(8,128)(2,1)S(1)}, bf16[40,3264]{1,0:T(8,128)(2,1)}, u32[]{:S(2)}, u32[]{:S(2)}) collective-permute-start(bf16[40,3264]{1,0:T(8,128)(2,1)S(1)} %get-tuple-element.50), channel_id=1, source_target_pairs={{0,3},{1,4},{2,5},{3,6},{4,7},{5,8},{6,9},{7,10},{8,11},{9,12},{10... | collective-permute-start | bytes 783368
  1136.6 68.2 %collective-permute-start.1 = (bf16[40,3264]{1,0:T(8,128)(2,1)S(1)}, bf16[40,3264]{1,0:T(8,128)(2,1)}, u32[]{:S(2)}, u32[]{:S(2)}) collective-permute-start(bf16[40,3264]{1,0:T(8,128)(2,1)S(1)} %get-tuple-element.50), channel_id=1, source_target_pairs={{0,2},{1,3},{2,4},{3,5},{4,6},{5,7},{6,8},{7,9},{8,10},{9,11},{10,... | collective-permute-start | bytes 783368
  1138.6 70.9 %collective-permute-start = (bf16[40,3264]{1,0:T(8,128)(2,1)S(1)}, bf16[40,3264]{1,0:T(8,128)(2,1)}, u32[]{:S(2)}, u32[]{:S(2)}) collective-permute-start(bf16[40,3264]{1,0:T(8,128)(2,1)S(1)} %get-tuple-element.50), channel_id=1, source_target_pairs={{0,1},{1,2},{2,3},{3,4},{4,5},{5,6},{6,7},{7,8},{8,9},{9,10},{10,1... | collective-permute-start | bytes 783368
  1142.2 36.2 %collective-permute-start.5 = (bf16[48,1088]{1,0:T(8,128)(2,1)S(1)}, bf16[48,1088]{1,0:T(8,128)(2,1)}, u32[]{:S(2)}, u32[]{:S(2)}) collective-permute-start(bf16[48,1088]{1,0:T(8,128)(2,1)S(1)} %get-tuple-element.51), channel_id=1, source_target_pairs={{0,1},{1,2},{2,3},{3,4},{4,5},{5,6},{6,7},{7,8},{8,9},{9,10},{10,1... | collective-permute-start | bytes 313352
  1178.4 19.5 %collective-permute-start.4 = (bf16[26,3264]{1,0:T(8,128)(2,1)S(1)}, bf16[26,3264]{1,0:T(8,128)(2,1)S(1)}, u32[]{:S(2)}, u32[]{:S(2)}) collective-permute-start(bf16[26,3264]{1,0:T(8,128)(2,1)S(1)} %slice.44), channel_id=1, source_target_pairs={{0,5},{1,6},{2,7},{3,8},{4,9},{5,10},{6,11},{7,12},{8,13},{9,14},{... | collective-permute-start | bytes 509192
  1197.8 87.7 %reduce-scatter.25.cloned.1.call-start = ((), (), s32[]{:S(2)}) async-start(), calls=%async_computation.9 | async-start | bytes 1044480
  1197.9 39.1 %collective-permute-start.18 = (bf16[40,4352]{1,0:T(8,128)(2,1)S(1)}, bf16[40,4352]{1,0:T(8,128)(2,1)S(1)}, u32[]{:S(2)}, u32[]{:S(2)}) collective-permute-start(bf16[40,4352]{1,0:T(8,128)(2,1)S(1)} %get-tuple-element.52), channel_id=1, source_target_pairs={{0,4},{1,5},{2,6},{3,7},{4,8},{5,9},{6,10},{7,11},{8,12},{9,13},{1... | collective-permute-start | bytes 1044488
  1199.2 37.7 %collective-permute-start.17 = (bf16[40,4352]{1,0:T(8,128)(2,1)S(1)}, bf16[40,4352]{1,0:T(8,128)(2,1)S(1)}, u32[]{:S(2)}, u32[]{:S(2)}) collective-permute-start(bf16[40,4352]{1,0:T(8,128)(2,1)S(1)} %get-tuple-element.52), channel_id=1, source_target_pairs={{0,3},{1,4},{2,5},{3,6},{4,7},{5,8},{6,9},{7,10},{8,11},{9,12},{10... | collective-permute-start | bytes 1044488
  1201.5 35.5 %collective-permute-start.16 = (bf16[40,4352]{1,0:T(8,128)(2,1)S(1)}, bf16[40,4352]{1,0:T(8,128)(2,1)}, u32[]{:S(2)}, u32[]{:S(2)}) collective-permute-start(bf16[40,4352]{1,0:T(8,128)(2,1)S(1)} %get-tuple-element.52), channel_id=1, source_target_pairs={{0,2},{1,3},{2,4},{3,5},{4,6},{5,7},{6,8},{7,9},{8,10},{9,11},{10,... | collective-permute-start | bytes 1044488
  1204.8 32.2 %collective-permute-start.15 = (bf16[40,4352]{1,0:T(8,128)(2,1)S(1)}, bf16[40,4352]{1,0:T(8,128)(2,1)}, u32[]{:S(2)}, u32[]{:S(2)}) collective-permute-start(bf16[40,4352]{1,0:T(8,128)(2,1)S(1)} %get-tuple-element.52), channel_id=1, source_target_pairs={{0,1},{1,2},{2,3},{3,4},{4,5},{5,6},{6,7},{7,8},{8,9},{9,10},{10,1... | collective-permute-start | bytes 1044488
  1209.5 27.4 %collective-permute-start.19 = (bf16[26,4352]{1,0:T(8,128)(2,1)}, bf16[26,4352]{1,0:T(8,128)(2,1)}, u32[]{:S(2)}, u32[]{:S(2)}) collective-permute-start(bf16[26,4352]{1,0:T(8,128)(2,1)} %slice.46), channel_id=1, source_target_pairs={{0,5},{1,6},{2,7},{3,8},{4,9},{5,10},{6,11},{7,12},{8,13},{9,14},{... | collective-permute-start | bytes 678920
  1236.9 64.6 %reduce-scatter.29.cloned.1.call-start = ((), (), s32[]{:S(2)}) async-start(), calls=%async_computation.11 | async-start | bytes 1392640
  1262.0 71.0 %reduce-scatter.31.cloned.1.call-start = ((), (), s32[]{:S(2)}) async-start(), calls=%async_computation.12 | async-start | bytes 696320
  (25 other events, 617.4 us)
Sparse Core Ops, SparseCore 0:
  10.2 319.9 all-gather.12
  332.4 142.6 all-gather.14
  476.8 168.8 all-gather.16
  648.0 233.4 reduce-scatter.32
  1198.0 34.4 reduce-scatter.26
  1237.0 30.2 reduce-scatter.24
  1270.0 31.5 reduce-scatter.28
  1304.7 28.1 reduce-scatter.30
